TPU v7x, 32 devices: a whole 2x2x4 slice. The times are simulated.
32 devices in a mesh: scene: 2 (over y), aper: 8 (over z, x), range: 2 (over core).
Axes of the slice: x: 2, y: 2, z: 4, core: 2. Of those that a mesh axis runs over, the one named last changes fastest.
Arguments:
- images: bfloat16 [16, 2, 512, 256], P(('scene', 'aper'), None, None, 'range'), parts along dimension 0, may hold values from -6 to 6
- interp_matrix: bfloat16 [1024, 512], replicated, may hold values from -0.25 to 0.25
- offsets: int32 [3, 2, 1024], replicated, may hold values from -28 to 28, as said below
- tap_index: int32 [3, 2, 1024], replicated, may hold values from 0 to 15
- tap_table: float32 [16, 8], replicated, may hold values from -1.5 to 1.5
- phase_base: float32 [3, 2, 1024], replicated, may hold values from -3.140625 to 3.140625
- phase_slope: float32 [3, 2, 1024], replicated, may hold values from -0.5 to 0.5
Outputs:
- merged: bfloat16 [16, 2, 512, 256], P(('scene', 'aper'), None, None, 'range'), parts along dimension 0
There are 2 independent parts, one for each index of `scene`. A program takes and returns all parts, laid end to end along the dimension named above; an argument that names none is the same for every part. Nothing has to cross between parts.
Inputs may be any that keep to these rules, and one draw needn't show every extreme that they name: `offsets`: for every level and role both -28 and 28 occur.
All inputs are finite; a program needn't handle non-finite values.
Results may differ from a plain program's by a relative error of at most 0.0085.
Values may be sent and summed in bfloat16 or wider, within the bound.
A program may use at most 64 MiB of HBM per device.

v0:
```python
import jax
import jax.numpy as jnp
from jax import lax
from jax.sharding import PartitionSpec as P

HALO = 32


def padded(cells, sides, width):
    for axis, dim in sides:
        count = lax.axis_size(axis)
        ends = count - 1
        head = lax.slice_in_dim(cells, 0, width, axis=dim)
        tail = lax.slice_in_dim(cells, cells.shape[dim] - width, cells.shape[dim], axis=dim)
        cells = jnp.concatenate(
            [
                lax.ppermute(tail, axis, [(i, (i + 1) % count) for i in range(ends)]),
                cells,
                lax.ppermute(head, axis, [((i + 1) % count, i) for i in range(ends)]),
            ],
            axis=dim,
        )
    return cells


def from_partner(value, axis, distance):
    mask = 2**distance
    pairs = [(source, source ^ mask) for source in range(lax.axis_size(axis))]
    return lax.ppermute(value, axis, pairs)


def interpolate(matrix_rows, image):
    return jnp.einsum("pa,can->cpn", matrix_rows, image, preferred_element_type=jnp.float32).astype(
        jnp.bfloat16
    )


def shifted(inter, shift_rows, tap_rows, first_col, out_width):
    taps_count = tap_rows.shape[1]
    needed = out_width + taps_count - 1
    total_width = inter.shape[2]
    start_cols = first_col - 3 + shift_rows
    moved = inter
    for bit_number in range((total_width - needed).bit_length()):
        stride_len = 1 << bit_number
        rolled = jnp.concatenate(
            [moved[:, :, stride_len:], jnp.zeros_like(moved[:, :, :stride_len])], axis=2
        )
        chosen_bits = start_cols >> bit_number & 1 == 1
        moved = jnp.where(chosen_bits[None, :, None], rolled, moved)
    window = moved[:, :, :needed]
    summed = jnp.zeros(window.shape[:2] + (out_width,), jnp.float32)
    for tap_number in range(taps_count):
        summed = summed + tap_rows[None, :, tap_number, None] * window[
            :, :, tap_number : tap_number + out_width
        ].astype(jnp.float32)
    return summed


def pick_rows(table, merge_level, child_role, own_half, angle_count):
    chosen = lax.dynamic_index_in_dim(table[merge_level], child_role, 0, keepdims=False)
    return lax.dynamic_slice_in_dim(chosen, own_half * angle_count, angle_count, 0)


def contribution(
    inter,
    merge_level,
    child_role,
    own_half,
    offsets,
    tap_index,
    tap_table,
    phase_base,
    phase_slope,
    out_width,
    anchor,
):
    angle_count = inter.shape[1]
    shift_rows = pick_rows(offsets, merge_level, child_role, own_half, angle_count)
    index_rows = pick_rows(tap_index, merge_level, child_role, own_half, angle_count)
    onehot = (
        index_rows[:, None] == jnp.arange(tap_table.shape[0], dtype=jnp.int32)[None, :]
    ).astype(jnp.float32)
    tap_rows = jnp.dot(
        onehot, tap_table, precision=lax.Precision.HIGHEST, preferred_element_type=jnp.float32
    )
    summed = shifted(inter, shift_rows, tap_rows, HALO, out_width)
    positions = (anchor + jnp.arange(out_width, dtype=jnp.int32)).astype(jnp.float32)
    base_rows = pick_rows(phase_base, merge_level, child_role, own_half, angle_count)
    slope_rows = pick_rows(phase_slope, merge_level, child_role, own_half, angle_count)
    phase_angle = base_rows[:, None] + slope_rows[:, None] * positions[None, :]
    cosine = jnp.cos(phase_angle)
    sine_part = jnp.sin(phase_angle)
    real_part = summed[0]
    imag_part = summed[1]
    return jnp.stack(
        [real_part * cosine - imag_part * sine_part, real_part * sine_part + imag_part * cosine]
    )


def body(images, interp_matrix, offsets, tap_index, tap_table, phase_base, phase_slope):
    current = images[0]
    angle_count = current.shape[1]
    shard_span = current.shape[2]
    levels = offsets.shape[0]
    aper_index = lax.axis_index("aper")
    range_index = lax.axis_index("range")
    scene_span = shard_span * lax.axis_size("range")
    current = padded(current, (("range", 2),), levels * HALO)
    for merge_level in range(levels):
        own_half = aper_index >> merge_level & 1
        margin = (levels - merge_level) * HALO
        extended = current
        out_width = extended.shape[2] - 2 * HALO
        anchor = range_index * shard_span - (margin - HALO)
        own_rows = lax.dynamic_slice_in_dim(interp_matrix, own_half * angle_count, angle_count, 0)
        partner = from_partner(extended, "aper", merge_level)
        own_inter = interpolate(own_rows, extended)
        received = interpolate(own_rows, partner)
        summed = contribution(
            own_inter,
            merge_level,
            own_half,
            own_half,
            offsets,
            tap_index,
            tap_table,
            phase_base,
            phase_slope,
            out_width,
            anchor,
        )
        summed = summed + contribution(
            received,
            merge_level,
            1 - own_half,
            own_half,
            offsets,
            tap_index,
            tap_table,
            phase_base,
            phase_slope,
            out_width,
            anchor,
        )
        if margin > HALO:
            positions = anchor + jnp.arange(out_width, dtype=jnp.int32)
            inside = (positions >= 0) & (positions < scene_span)
            summed = jnp.where(inside[None, None, :], summed, 0.0)
        current = summed.astype(jnp.bfloat16)
    return current[None]


def solution(mesh):
    return jax.shard_map(
        body,
        mesh=mesh,
        in_specs=(P(("scene", "aper"), None, None, "range"), P(), P(), P(), P(), P(), P()),
        out_specs=P(("scene", "aper"), None, None, "range"),
        check_vma=False,
    )
```

profile of v0, /device:TPU:0, one launch (start us, length us, event | category | flops | bytes accessed | tf_op | source)
XLA Modules:
  0.0 82.5 jit_solution(4897862011869639215)
XLA Ops:
  0.0 1.2 %copy.8 = bf16[1,2,512,128]{2,3,1,0:T(8,128)(2,1)S(1)} copy(bf16[1,2,512,128]{3,2,1,0:T(8,128)(2,1)} %param.7) | data formatting | bytes 524288 | tf_op args[0]
  1.2 2.4 %collective-permute-start = (bf16[2,512,96]{1,2,0:T(8,128)(2,1)S(1)}, bf16[2,512,96]{1,2,0:T(8,128)(2,1)S(1)}, u32[]{:S(2)}, u32[]{:S(2)}) collective-permute-start(bf16[2,512,96]{1,2,0:T(8,128)(2,1)S(1)} %get-tuple-element.53), channel_id=1, source_target_pairs={{0,1},{2,3},{4,5},{6,7},{8,9},{10,11},{12,13},{14,15},{16,17},{18,... | collective-permute-start | bytes 589832 | tf_op jit(solution)/shard_map/ppermute | solution.py:17
  3.7 1.3 %collective-permute-start.1 = (bf16[2,512,96]{1,2,0:T(8,128)(2,1)S(1)}, bf16[2,512,96]{1,2,0:T(8,128)(2,1)S(1)}, u32[]{:S(2)}, u32[]{:S(2)}) collective-permute-start(bf16[2,512,96]{1,2,0:T(8,128)(2,1)S(1)} %get-tuple-element.54), channel_id=1, source_target_pairs={{1,0},{3,2},{5,4},{7,6},{9,8},{11,10},{13,12},{15,14},{17,16},{19,... | collective-permute-start | bytes 589832 | tf_op jit(solution)/shard_map/ppermute | solution.py:19
  5.3 0.3 fusion.37
  5.7 0.3 fusion.38
  6.3 0.3 fusion.36
  6.7 0.3 fusion.39
  7.2 0.3 fusion.35
  7.6 0.3 fusion.40
  8.4 0.5 fusion
  8.9 0.2 slice.703
  9.1 0.2 pad_select_fusion.11
  9.4 0.2 pad_select_fusion.10
  9.6 0.2 slice.705
  9.8 0.2 pad_select_fusion.9
  10.0 0.2 pad_select_fusion.8
  10.2 0.2 pad_select_fusion.7
  10.5 2.4 %collective-permute-start.2 = (bf16[2,512,320]{1,2,0:T(8,128)(2,1)S(1)}, bf16[2,512,320]{1,2,0:T(8,128)(2,1)S(1)}, u32[]{:S(2)}, u32[]{:S(2)}) collective-permute-start(bf16[2,512,320]{1,2,0:T(8,128)(2,1)S(1)} %pad_maximum_fusion), channel_id=1, source_target_pairs={{0,2},{2,0},{4,6},{6,4},{8,10},{10,8},{12,14},{14,12},{1,3},{3,1},... | collective-permute-start | bytes 1966088 | tf_op jit(solution)/shard_map/ppermute | solution.py:29
  12.9 0.2 pad_select_fusion.6
  13.1 1.0 %multiply_add_fusion.1 = f32[2,512,256]{1,2,0:T(8,128)S(1)} fusion(bf16[2,512,320]{1,2,0:T(8,128)(2,1)S(1)} %pad_select_fusion.6, f32[512]{0:T(512)S(1)} %bitcast.125, f32[512]{0:T(512)S(1)} %bitcast.126, f32[512]{0:T(512)S(1)} %bitcast.127, f32[512]{0:T(512)S(1)} %bitcast.128, f32[512]{0:T(512)S(1)} %bitcast.129, f32[512]{0:T(512)S(1)} %bitcast.130, ...), kind=kLoop, calls=%fused_computation.16 | loop fusion | flops 6029312 | bytes 5259264 | tf_op jit(solution)/shard_map/add | solution.py:54
  14.1 13.9 %collective-permute-done.2 = bf16[2,512,320]{1,2,0:T(8,128)(2,1)S(1)} collective-permute-done((bf16[2,512,320]{1,2,0:T(8,128)(2,1)S(1)}, bf16[2,512,320]{1,2,0:T(8,128)(2,1)S(1)}, u32[]{:S(2)}, u32[]{:S(2)}) %collective-permute-start.2) | collective-permute-done | bytes 655392 | tf_op jit(solution)/shard_map/ppermute | solution.py:29
  28.0 0.5 fusion.1
  28.6 0.2 slice.727
  28.7 0.2 pad_select_fusion.5
  29.1 0.2 pad_select_fusion.4
  29.4 0.2 pad_select_fusion.3
  29.7 0.2 pad_select_fusion.2
  29.9 0.2 pad_select_fusion.1
  30.1 0.2 pad_select_fusion
  30.3 1.0 %multiply_add_fusion = f32[2,512,256]{1,2,0:T(8,128)S(1)} fusion(bf16[2,512,320]{1,2,0:T(8,128)(2,1)S(1)} %pad_select_fusion, f32[512]{0:T(512)S(1)} %bitcast.117, f32[512]{0:T(512)S(1)} %bitcast.118, f32[512]{0:T(512)S(1)} %bitcast.119, f32[512]{0:T(512)S(1)} %bitcast.120, f32[512]{0:T(512)S(1)} %bitcast.121, f32[512]{0:T(512)S(1)} %bitcast.122, ...), kind=kLoop, calls=%fused_computation.15 | loop fusion | flops 6029312 | bytes 5259264 | tf_op jit(solution)/shard_map/add | solution.py:54
  31.3 4.4 %multiply_subtract_fusion = (f32[1,512,256]{1,2,0:T(8,128)S(1)}, f32[1,512,256]{1,2,0:T(8,128)S(1)}, f32[1,512,256]{1,2,0:T(8,128)S(1)}, f32[1,512,256]{1,2,0:T(8,128)S(1)}) fusion(f32[2,512,256]{1,2,0:T(8,128)S(1)} %multiply_add_fusion, f32[512]{0:T(512)S(1)} %bitcast.168, f32[512]{0:T(512)S(1)} %bitcast.171, f32[256]{0:T(256)S(1)} %fusion.59, ...), kind=kLoop, calls=%fused_computation.58 | loop fusion | flops 2097152 | bytes 4203520 | tf_op jit(solution)/shard_map/sub | solution.py:97
  35.8 0.2 fusion.7
  36.0 0.5 fusion.2
  36.5 2.4 %collective-permute-start.3 = (bf16[2,512,256]{1,2,0:T(8,128)(2,1)S(1)}, bf16[2,512,256]{1,2,0:T(8,128)(2,1)S(1)}, u32[]{:S(2)}, u32[]{:S(2)}) collective-permute-start(bf16[2,512,256]{1,2,0:T(8,128)(2,1)S(1)} %fusion.7), channel_id=1, source_target_pairs={{0,4},{2,6},{4,0},{6,2},{8,12},{10,14},{12,8},{14,10},{1,5},{3,7},... | collective-permute-start | bytes 1572872 | tf_op jit(solution)/shard_map/ppermute | solution.py:29
  40.3 0.8 multiply_add_fusion.3
  41.0 10.1 %collective-permute-done.3 = bf16[2,512,256]{1,2,0:T(8,128)(2,1)S(1)} collective-permute-done((bf16[2,512,256]{1,2,0:T(8,128)(2,1)S(1)}, bf16[2,512,256]{1,2,0:T(8,128)(2,1)S(1)}, u32[]{:S(2)}, u32[]{:S(2)}) %collective-permute-start.3) | collective-permute-done | bytes 524320 | tf_op jit(solution)/shard_map/ppermute | solution.py:29
  51.1 0.5 fusion.3
  53.0 0.8 multiply_add_fusion.2
  53.7 3.2 %multiply_subtract_fusion.2 = (f32[1,512,192]{1,2,0:T(8,128)S(1)}, f32[1,512,192]{1,2,0:T(8,128)S(1)}, f32[1,512,192]{1,2,0:T(8,128)S(1)}, f32[1,512,192]{1,2,0:T(8,128)S(1)}) fusion(f32[2,512,192]{1,2,0:T(8,128)S(1)} %multiply_add_fusion.2, f32[512]{0:T(512)S(1)} %bitcast.172, f32[512]{0:T(512)S(1)} %bitcast.175, f32[192]{0:T(256)S(1)} %fusion.60, ...), kind=kLoop, calls=%fused_computation.86 | loop fusion | flops 1572864 | bytes 3154688 | tf_op jit(solution)/shard_map/sub | solution.py:97
  56.9 0.2 fusion.9
  57.1 0.4 fusion.4
  57.5 2.8 %collective-permute-start.4 = (bf16[2,512,192]{1,2,0:T(8,128)(2,1)S(1)}, bf16[2,512,192]{1,2,0:T(8,128)(2,1)S(1)}, u32[]{:S(2)}, u32[]{:S(2)}) collective-permute-start(bf16[2,512,192]{1,2,0:T(8,128)(2,1)S(1)} %fusion.9), channel_id=1, source_target_pairs={{0,8},{2,10},{4,12},{6,14},{8,0},{10,2},{12,4},{14,6},{1,9},{3,11}... | collective-permute-start | bytes 1179656 | tf_op jit(solution)/shard_map/ppermute | solution.py:29
  61.4 0.5 multiply_add_fusion.5
  61.9 15.6 %collective-permute-done.4 = bf16[2,512,192]{1,2,0:T(8,128)(2,1)S(1)} collective-permute-done((bf16[2,512,192]{1,2,0:T(8,128)(2,1)S(1)}, bf16[2,512,192]{1,2,0:T(8,128)(2,1)S(1)}, u32[]{:S(2)}, u32[]{:S(2)}) %collective-permute-start.4) | collective-permute-done | bytes 393248 | tf_op jit(solution)/shard_map/ppermute | solution.py:29
  77.5 0.4 fusion.5
  78.9 0.5 multiply_add_fusion.4
  79.4 2.1 %subtract_bitcast_fusion = (f32[1,1,512,128]{2,3,1,0:T(8,128)S(1)}, f32[1,1,512,128]{2,3,1,0:T(8,128)S(1)}, f32[1,1,512,128]{2,3,1,0:T(8,128)S(1)}, f32[1,1,512,128]{2,3,1,0:T(8,128)S(1)}) fusion(f32[2,512,128]{1,2,0:T(8,128)S(1)} %multiply_add_fusion.4, f32[512]{0:T(512)S(1)} %bitcast.132, f32[512]{0:T(512)S(1)} %bitcast.135, f32[128]{0:T(128)S(1)} %add_convert_fusion, ...), kind=kLoop, calls=%fused_computation.96 | loop fusion | flops 1048576 | bytes 2105856 | tf_op jit(solution)/shard_map/stack | solution.py:96
  81.7 0.8 %copy.9 = bf16[1,2,512,128]{3,2,1,0:T(8,128)(2,1)} copy(bf16[1,2,512,128]{2,3,1,0:T(8,128)(2,1)S(1)} %fusion.10) | data formatting | bytes 524288 | tf_op jit(solution)/shard_map/convert_element_type | solution.py:150
  (102 shorter events, 6.6 us)
Async XLA Ops:
  0.0 8.4 %copy-start = (bf16[1024,512]{1,0:T(8,128)(2,1)S(1)}, bf16[1024,512]{1,0:T(8,128)(2,1)}, u32[]{:S(2)}) copy-start(bf16[1024,512]{1,0:T(8,128)(2,1)} %param.8) | copy-start | bytes 3145732
  0.0 5.1 %copy-start.1 = (s32[3,2,1024]{2,1,0:T(2,128)S(1)}, s32[3,2,1024]{2,1,0:T(2,128)}, u32[]{:S(2)}) copy-start(s32[3,2,1024]{2,1,0:T(2,128)} %param.10) | copy-start | bytes 73732
  0.0 5.1 %copy-start.2 = (s32[3,2,1024]{2,1,0:T(2,128)S(1)}, s32[3,2,1024]{2,1,0:T(2,128)}, u32[]{:S(2)}) copy-start(s32[3,2,1024]{2,1,0:T(2,128)} %param.9) | copy-start | bytes 73732
  0.0 5.3 %copy-start.5 = (f32[16,8]{0,1:T(8,128)S(1)}, f32[16,8]{0,1:T(8,128)}, u32[]{:S(2)}) copy-start(f32[16,8]{0,1:T(8,128)} %param.11) | copy-start | bytes 1540
  0.0 6.0 %copy-start.3 = (f32[3,2,1024]{2,1,0:T(2,128)S(1)}, f32[3,2,1024]{2,1,0:T(2,128)}, u32[]{:S(2)}) copy-start(f32[3,2,1024]{2,1,0:T(2,128)} %param.12) | copy-start | bytes 73732
  0.0 6.0 %copy-start.4 = (f32[3,2,1024]{2,1,0:T(2,128)S(1)}, f32[3,2,1024]{2,1,0:T(2,128)}, u32[]{:S(2)}) copy-start(f32[3,2,1024]{2,1,0:T(2,128)} %param.13) | copy-start | bytes 73732
  1.2 7.1 %collective-permute-start = (bf16[2,512,96]{1,2,0:T(8,128)(2,1)S(1)}, bf16[2,512,96]{1,2,0:T(8,128)(2,1)S(1)}, u32[]{:S(2)}, u32[]{:S(2)}) collective-permute-start(bf16[2,512,96]{1,2,0:T(8,128)(2,1)S(1)} %get-tuple-element.53), channel_id=1, source_target_pairs={{0,1},{2,3},{4,5},{6,7},{8,9},{10,11},{12,13},{14,15},{16,17},{18,... | collective-permute-start | bytes 589832 | tf_op jit(solution)/shard_map/ppermute | solution.py:17
  3.7 4.7 %collective-permute-start.1 = (bf16[2,512,96]{1,2,0:T(8,128)(2,1)S(1)}, bf16[2,512,96]{1,2,0:T(8,128)(2,1)S(1)}, u32[]{:S(2)}, u32[]{:S(2)}) collective-permute-start(bf16[2,512,96]{1,2,0:T(8,128)(2,1)S(1)} %get-tuple-element.54), channel_id=1, source_target_pairs={{1,0},{3,2},{5,4},{7,6},{9,8},{11,10},{13,12},{15,14},{17,16},{19,... | collective-permute-start | bytes 589832 | tf_op jit(solution)/shard_map/ppermute | solution.py:19
  10.5 17.5 %collective-permute-start.2 = (bf16[2,512,320]{1,2,0:T(8,128)(2,1)S(1)}, bf16[2,512,320]{1,2,0:T(8,128)(2,1)S(1)}, u32[]{:S(2)}, u32[]{:S(2)}) collective-permute-start(bf16[2,512,320]{1,2,0:T(8,128)(2,1)S(1)} %pad_maximum_fusion), channel_id=1, source_target_pairs={{0,2},{2,0},{4,6},{6,4},{8,10},{10,8},{12,14},{14,12},{1,3},{3,1},... | collective-permute-start | bytes 1966088 | tf_op jit(solution)/shard_map/ppermute | solution.py:29
  36.5 14.6 %collective-permute-start.3 = (bf16[2,512,256]{1,2,0:T(8,128)(2,1)S(1)}, bf16[2,512,256]{1,2,0:T(8,128)(2,1)S(1)}, u32[]{:S(2)}, u32[]{:S(2)}) collective-permute-start(bf16[2,512,256]{1,2,0:T(8,128)(2,1)S(1)} %fusion.7), channel_id=1, source_target_pairs={{0,4},{2,6},{4,0},{6,2},{8,12},{10,14},{12,8},{14,10},{1,5},{3,7},... | collective-permute-start | bytes 1572872 | tf_op jit(solution)/shard_map/ppermute | solution.py:29
  57.5 19.9 %collective-permute-start.4 = (bf16[2,512,192]{1,2,0:T(8,128)(2,1)S(1)}, bf16[2,512,192]{1,2,0:T(8,128)(2,1)S(1)}, u32[]{:S(2)}, u32[]{:S(2)}) collective-permute-start(bf16[2,512,192]{1,2,0:T(8,128)(2,1)S(1)} %fusion.9), channel_id=1, source_target_pairs={{0,8},{2,10},{4,12},{6,14},{8,0},{10,2},{12,4},{14,6},{1,9},{3,11}... | collective-permute-start | bytes 1179656 | tf_op jit(solution)/shard_map/ppermute | solution.py:29
where the time goes:
time: 82.7 us; the launch traced here: 82.5 us
  waiting for transfers between devices  39.6 us (48%)
  other arithmetic  20.4 us (25%)
  starting transfers between devices  11.4 us (14%)
  local copies, waits for them, and re-layouts  5.49 us (7%)
  matrix products  4.68 us (6%)
  between operations  1 us (1%)
    ppermute x3, waiting for transfers between devices, from_partner(): return lax.ppermute(value, axis, pairs)  39.6 us
    ppermute x3, starting transfers between devices, from_partner(): return lax.ppermute(value, axis, pairs)  7.65 us
    sub x2, other arithmetic, contribution(): real_part * cosine - imag_part * sine_part  7.62 us
    select_n x36, other arithmetic, shifted(): moved = jnp.where(chosen_bits[None, :, None], rolled, moved)  4.95 us
    add x6, other arithmetic, shifted(): summed + tap_rows[None, :, tap_number, None] * window[:, :, tap_number:ta...  4.62 us
    dot_general x6, matrix products, interpolate(): jnp.einsum('pa,can->cpn', matrix_rows, image, preferred_element_type=jnp....  2.82 us
    slice x36, local copies, waits for them, and re-layouts, shifted(): moved[:, :, stride_len:]  2.81 us
    ppermute x1, starting transfers between devices, padded(): lax.ppermute(tail, axis, [(i, (i + 1) % count) for i in range(ends)])  2.42 us
  transfers between devices with their start and end apart: 5, of which 3 were waited for; matrix products, arithmetic and copies ran while one was open for 9% of the time, Pallas kernels for 0%

commit v1 on v0

v1 whole, which is shorter than its diff:
```python
import functools

import jax
import jax.numpy as jnp
from jax import lax
from jax.experimental import pallas as pl
from jax.experimental.pallas import tpu as pltpu
from jax.sharding import PartitionSpec as P

MESH = pl.DeviceIdType.MESH
LANES = 128
GROUP = 16
BLOCKS = 4
CHUNKS = 2
F32 = jnp.float32
BF16 = jnp.bfloat16


def sincos(angle):
    turns = jnp.floor(angle * 0.6366197723675814 + 0.5)
    rest = angle - turns * 1.5703125
    rest = rest - turns * 4.837512969970703125e-4
    rest = rest - turns * 7.54978995489188216e-8
    quadrant = turns.astype(jnp.int32)
    square = rest * rest
    sine = rest + rest * square * (
        -1.6666654611e-1 + square * (8.3321608736e-3 + square * -1.9515295891e-4)
    )
    cosine = (1.0 - 0.5 * square) + square * square * (
        4.166664568298827e-2 + square * (-1.388731625493765e-3 + square * 2.443315711809948e-5)
    )
    odd = (quadrant & 1) == 1
    swapped_sine = jnp.where(odd, cosine, sine)
    swapped_cosine = jnp.where(odd, sine, cosine)
    sine = jnp.where((quadrant & 2) == 2, -swapped_sine, swapped_sine)
    cosine = jnp.where(((quadrant + 1) & 2) == 2, -swapped_cosine, swapped_cosine)
    return sine, cosine


def kernel(
    levels,
    cores,
    images,
    matrix,
    offsets,
    tap_index,
    tap_table,
    phase_base,
    phase_slope,
    out,
    image,
    rows_of,
    params,
    outgoing,
    incoming,
    mine,
    waves,
    handed,
    local_sem,
    first_sem,
    inter_sem,
    merge_sem,
):
    angles = image.shape[2]
    width = image.shape[3]
    span = width // cores
    pieces = width // LANES
    share = angles // cores
    rows = share // BLOCKS
    chunk = share // CHUNKS
    taps = tap_table.shape[1]
    scene = lax.axis_index("scene")
    aper = lax.axis_index("aper")
    core = lax.axis_index("range")
    first_row = pl.multiple_of(core * share, share)
    halves = [lax.rem(aper // 2**level, 2) for level in range(levels)]
    partners = [aper + (1 - 2 * halves[level]) * 2**level for level in range(levels)]
    others = [lax.rem(core + step, cores) for step in range(1, cores)]

    barrier = pltpu.get_barrier_semaphore()
    for partner in partners:
        pl.semaphore_signal(barrier, inc=1, device_id=(scene, partner, core), device_id_type=MESH)
    for other in others:
        pl.semaphore_signal(barrier, inc=1, device_id=(scene, aper, other), device_id_type=MESH)

    own_columns = pl.ds(pl.multiple_of(core * span, span), span)
    local_copies = [
        pltpu.make_async_copy(
            images.at[0], image.at[0, :, :, own_columns], local_sem.at[0]
        )
    ]
    for half in range(2):
        local_copies.append(
            pltpu.make_async_copy(
                matrix.at[pl.ds(half * angles + first_row, share), :],
                rows_of.at[half],
                local_sem.at[1 + half],
            )
        )
    for copy in local_copies:
        copy.start()

    def build_params(level):
        picked = pl.ds(pl.multiple_of(halves[level] * angles + core * share, LANES), share)
        index = tap_index[level, :, picked]
        weights = [jnp.zeros(index.shape, F32) for _ in range(taps)]
        for entry in range(tap_table.shape[0]):
            hit = index == entry
            for tap in range(taps):
                weights[tap] = jnp.where(hit, tap_table[entry, tap], weights[tap])
        start = offsets[level, :, picked].astype(F32) - 3.0
        base = phase_base[level, :, picked]
        slope = phase_slope[level, :, picked]
        for role in range(2):
            lines = [line[role : role + 1] for line in weights + [start, base, slope]]
            lines.append(jnp.zeros((LANES - len(lines), share), F32))
            params[level, role] = jnp.concatenate(lines, axis=0).T

    def wave(level, role, where):
        table = params[level, role, where, :]
        base = table[:, taps + 1 : taps + 2]
        slope = table[:, taps + 2 : taps + 3]
        lane = lax.broadcasted_iota(jnp.int32, (GROUP, LANES), 1).astype(F32)
        return [sincos(base + slope * (lane + float(LANES * piece))) for piece in range(pieces)]

    def term(level, role, where, parts, trig):
        table = params[level, role, where, :]
        lane = lax.broadcasted_iota(jnp.int32, (GROUP, LANES), 1)
        place = lane + table[:, taps : taps + 1].astype(jnp.int32)
        before = place < 0
        after = place >= LANES
        source = place & (LANES - 1)
        weights = [
            jnp.broadcast_to(table[:, tap : tap + 1], (GROUP, LANES)) for tap in range(taps)
        ]
        zero = jnp.zeros((GROUP, LANES), F32)
        shifted = []
        for part in parts:
            turned = [zero]
            for piece in range(pieces):
                value = part[:, piece * LANES : (piece + 1) * LANES].astype(F32)
                turned.append(
                    jnp.take_along_axis(value, source, axis=1, mode="promise_in_bounds")
                )
            turned += [zero, zero]
            window = [
                jnp.where(before, turned[piece], jnp.where(after, turned[piece + 2], turned[piece + 1]))
                for piece in range(pieces + 1)
            ]
            sums = []
            for piece in range(pieces):
                total = weights[0] * window[piece]
                for tap in range(1, taps):
                    mixed = jnp.where(lane >= tap, window[piece], window[piece + 1])
                    total = total + weights[tap] * pltpu.roll(mixed, LANES - tap, 1)
                sums.append(total)
            shifted.append(sums)
        real, imag = [], []
        for piece in range(pieces):
            sine, cosine = trig[piece]
            real.append(shifted[0][piece] * cosine - shifted[1][piece] * sine)
            imag.append(shifted[0][piece] * sine + shifted[1][piece] * cosine)
        return real, imag

    build_params(0)
    pl.semaphore_wait(barrier, len(partners) + len(others))

    first_copies = []
    for position, other in enumerate(others):
        copy = pltpu.make_async_remote_copy(
            src_ref=images.at[0],
            dst_ref=image.at[0, :, :, own_columns],
            send_sem=first_sem.at[0, position],
            recv_sem=first_sem.at[1, position],
            device_id=(scene, aper, other),
            device_id_type=MESH,
        )
        copy.start()
        first_copies.append(copy)
    for copy in local_copies:
        copy.wait()
    for copy in first_copies:
        copy.wait()

    def block_rows(block):
        return pl.ds(pl.multiple_of(block * rows, rows), rows)

    def inter_copy(level, block):
        picked = block_rows(block)
        return pltpu.make_async_remote_copy(
            src_ref=outgoing.at[level, :, picked, :],
            dst_ref=incoming.at[level, :, picked, :],
            send_sem=inter_sem.at[0, level, block],
            recv_sem=inter_sem.at[1, level, block],
            device_id=(scene, partners[level], core),
            device_id_type=MESH,
        )

    def merge_copy(level, block, position):
        picked = pl.ds(pl.multiple_of(first_row + block * rows, rows), rows)
        if level + 1 < levels:
            source = image.at[level + 1, :, picked, :]
            target = source
        else:
            source = handed.at[position, :, block_rows(block), :]
            target = out.at[0, :, picked, :]
        return pltpu.make_async_remote_copy(
            src_ref=source,
            dst_ref=target,
            send_sem=merge_sem.at[0, level, position, block],
            recv_sem=merge_sem.at[1, level, position, block],
            device_id=(scene, aper, others[position]),
            device_id_type=MESH,
        )

    for level in range(levels):
        half = halves[level]
        for piece in range(CHUNKS):
            picked = pl.ds(piece * chunk, chunk)
            for part in range(2):
                outgoing[level, part, picked, :] = jnp.dot(
                    rows_of[1 - half, picked, :], image[level, part], preferred_element_type=F32
                ).astype(BF16)
            for block in range(piece * BLOCKS // CHUNKS, (piece + 1) * BLOCKS // CHUNKS):
                inter_copy(level, block).start()

        for part in range(2):
            mine[part] = jnp.dot(
                rows_of[half], image[level, part], preferred_element_type=F32
            )
        if level + 1 < levels:
            build_params(level + 1)

        @pl.loop(0, share // GROUP)
        def _(group):
            where = pl.ds(pl.multiple_of(group * GROUP, GROUP), GROUP)
            parts = [mine[part, where, :].astype(BF16) for part in range(2)]
            real, imag = term(level, half, where, parts, wave(level, half, where))
            trig = wave(level, 1 - half, where)
            for piece in range(pieces):
                columns = slice(piece * LANES, (piece + 1) * LANES)
                mine[0, where, columns] = real[piece]
                mine[1, where, columns] = imag[piece]
                waves[0, where, columns] = trig[piece][0]
                waves[1, where, columns] = trig[piece][1]

        @pl.loop(0, BLOCKS)
        def _(block):
            inter_copy(level, block).wait_recv()

            @pl.loop(0, rows // GROUP)
            def _(group):
                start = pl.multiple_of(block * rows + group * GROUP, GROUP)
                where = pl.ds(start, GROUP)
                target = pl.ds(pl.multiple_of(first_row + start, GROUP), GROUP)
                parts = [incoming[level, part, where, :] for part in range(2)]
                trig = []
                for piece in range(pieces):
                    columns = slice(piece * LANES, (piece + 1) * LANES)
                    trig.append((waves[0, where, columns], waves[1, where, columns]))
                sums = term(level, 1 - half, where, parts, trig)
                for part in range(2):
                    merged = [
                        (
                            mine[part, where, piece * LANES : (piece + 1) * LANES]
                            + sums[part][piece]
                        ).astype(BF16)
                        for piece in range(pieces)
                    ]
                    if level + 1 < levels:
                        for piece in range(pieces):
                            columns = slice(piece * LANES, (piece + 1) * LANES)
                            image[level + 1, part, target, columns] = merged[piece]
                    else:
                        per_core = pieces // cores
                        for slot in range(per_core):
                            columns = slice(slot * LANES, (slot + 1) * LANES)
                            for position, owner in enumerate([core] + others):
                                chosen = merged[slot].astype(F32)
                                for rank in range(1, cores):
                                    chosen = jnp.where(
                                        owner == rank,
                                        merged[rank * per_core + slot].astype(F32),
                                        chosen,
                                    )
                                if position == 0:
                                    out[0, part, target, columns] = chosen.astype(BF16)
                                else:
                                    handed[position - 1, part, where, columns] = chosen.astype(BF16)

            for position in range(len(others)):
                merge_copy(level, block, position).start()

        @pl.loop(0, BLOCKS)
        def _(block):
            for position in range(len(others)):
                copy = merge_copy(level, block, position)
                copy.wait_send()
                sender = lax.rem(core + cores - 1 - position, cores)
                picked = pl.ds(pl.multiple_of(sender * share + block * rows, rows), rows)
                landed = (
                    image.at[level + 1, :, picked, :]
                    if level + 1 < levels
                    else out.at[0, :, picked, :]
                )
                pltpu.make_async_remote_copy(
                    src_ref=landed,
                    dst_ref=landed,
                    send_sem=merge_sem.at[0, level, position, block],
                    recv_sem=merge_sem.at[1, level, position, block],
                    device_id=(scene, aper, sender),
                    device_id_type=MESH,
                ).wait_recv()

    for level in range(levels):

        @pl.loop(0, BLOCKS)
        def _(block):
            inter_copy(level, block).wait_send()


def body(images, interp_matrix, offsets, tap_index, tap_table, phase_base, phase_slope):
    cores = lax.axis_size("range")
    levels = offsets.shape[0]
    angles = images.shape[2]
    width = images.shape[3] * cores
    share = angles // cores
    vmem = pl.BlockSpec(memory_space=pltpu.VMEM)
    anywhere = pl.BlockSpec(memory_space=pl.ANY)
    return pl.pallas_call(
        functools.partial(kernel, levels, cores),
        out_shape=jax.ShapeDtypeStruct(images.shape, images.dtype),
        in_specs=[
            anywhere,
            anywhere,
            vmem,
            vmem,
            pl.BlockSpec(memory_space=pltpu.SMEM),
            vmem,
            vmem,
        ],
        out_specs=vmem,
        scratch_shapes=[
            pltpu.VMEM((levels, 2, angles, width), BF16),
            pltpu.VMEM((2, share, angles), BF16),
            pltpu.VMEM((levels, 2, share, LANES), F32),
            pltpu.VMEM((levels, 2, share, width), BF16),
            pltpu.VMEM((levels, 2, share, width), BF16),
            pltpu.VMEM((2, share, width), F32),
            pltpu.VMEM((2, share, width), F32),
            pltpu.VMEM((cores - 1, 2, share, images.shape[3]), BF16),
            pltpu.SemaphoreType.DMA((3,)),
            pltpu.SemaphoreType.DMA((2, cores - 1)),
            pltpu.SemaphoreType.DMA((2, levels, BLOCKS)),
            pltpu.SemaphoreType.DMA((2, levels, cores - 1, BLOCKS)),
        ],
        compiler_params=pltpu.CompilerParams(collective_id=0, has_side_effects=True),
    )(images, interp_matrix, offsets, tap_index, tap_table, phase_base, phase_slope)


def solution(mesh):
    return jax.shard_map(
        body,
        mesh=mesh,
        in_specs=(P(("scene", "aper"), None, None, "range"), P(), P(), P(), P(), P(), P()),
        out_specs=P(("scene", "aper"), None, None, "range"),
        check_vma=False,
    )
```

time: 82.7 us -> 47.5 us (0.57)
  Pallas kernels: 0 us -> 44.2 us
  waiting for transfers between devices: 39.6 us -> 0 us
  other arithmetic: 20.4 us -> 0 us
  starting transfers between devices: 11.4 us -> 0 us
  matrix products: 4.68 us -> 0 us
  local copies, waits for them, and re-layouts: 5.49 us -> 3.02 us
  between operations: 1 us -> 0.01 us
    pallas_call x0 -> x1, Pallas kernels: none -> 44.2 us  [body(): pl.pallas_call(functools.partial(kernel, levels, cores), out_shape=jax.Sh...]
    ppermute x5 -> x0, waiting for transfers between devices: 39.6 us -> none  [the longest x3 39.6 us: from_partner(): return lax.ppermute(value, axis, pairs)]
    ppermute x5 -> x0, starting transfers between devices: 11.4 us -> none  [the longest x3 7.65 us: from_partner(): return lax.ppermute(value, axis, pairs)]
    sub x2 -> x0, other arithmetic: 7.62 us -> none  [contribution(): real_part * cosine - imag_part * sine_part]
    select_n x36 -> x0, other arithmetic: 4.95 us -> none  [shifted(): moved = jnp.where(chosen_bits[None, :, None], rolled, moved)]
    add x8 -> x0, other arithmetic: 4.8 us -> none  [the longest x6 4.62 us: shifted(): summed + tap_rows[None, :, tap_number, None] * window[:, :, tap_number:ta...]
    dot_general x12 -> x0, matrix products: 4.68 us -> none  [the longest x6 2.82 us: interpolate(): jnp.einsum('pa,can->cpn', matrix_rows, image, preferred_element_type=jnp....]
    slice x47 -> x0, local copies, waits for them, and re-layouts: 3.01 us -> none  [the longest x36 2.81 us: shifted(): moved[:, :, stride_len:]]
  transfers between devices with their start and end apart: 5 -> 0, of which waited for: 3 -> 0; matrix products, arithmetic and copies ran while one was open for 9% -> 0% of each run, Pallas kernels for 0% -> 0%
where the time goes in v1:
time: 47.5 us; the launch traced here: 47.2 us
  Pallas kernels  44.2 us (93%)
  local copies, waits for them, and re-layouts  3.02 us (6%)
    pallas_call x1, Pallas kernels, body(): pl.pallas_call(functools.partial(kernel, levels, cores), out_shape=jax.Sh...  44.2 us
    unnamed x2, local copies, waits for them, and re-layouts  3.02 us

profile of v1, /device:TPU:0, one launch (start us, length us, event | category | flops | bytes accessed | tf_op | source)
XLA Modules:
  0.0 47.2 jit_solution(11226366949941056567)
XLA Ops:
  0.0 1.4 %copy.8.tap_table = f32[16,8]{1,0:T(8,128)} copy(f32[16,8]{0,1:T(8,128)} %param.11) | data formatting | bytes 1024 | tf_op args[4]
  1.4 44.2 %shard_map.73 = bf16[1,2,512,128]{3,2,1,0:T(8,128)(2,1)} custom-call(bf16[1,2,512,128]{3,2,1,0:T(8,128)(2,1)} %images.1, bf16[1024,512]{1,0:T(8,128)(2,1)} %matrix.1, s32[3,2,1024]{2,1,0:T(2,128)} %offsets.1, s32[3,2,1024]{2,1,0:T(2,128)} %tap_index.1, f32[16,8]{1,0:T(8,128)} %copy.8.tap_table, f32[3,2,1024]{2,1,0:T(2,128)} %phase_base.1, ...), custom_call_target="tpu_custom_call" | custom-call | tf_op jit(solution)/shard_map/pallas_call | solution.py:330
  45.5 1.7 %copy.10 = bf16[1,2,512,128]{3,2,1,0:T(8,128)(2,1)} copy(bf16[1,2,512,128]{3,2,1,0:T(8,128)(2,1)} %shard_map.73) | data formatting | bytes 524288

commit v2 on v0

v2 whole, which is shorter than its diff:
```python
import functools

import jax
import jax.numpy as jnp
from jax import lax
from jax.experimental import pallas as pl
from jax.experimental.pallas import tpu as pltpu
from jax.sharding import PartitionSpec as P

MESH = pl.DeviceIdType.MESH
LANES = 128
REACH = 32
FINE = 8
SEND_LAG = 2
MERGE_LAG = 7
F32 = jnp.float32
BF16 = jnp.bfloat16


def sincos(angle):
    turns = jnp.floor(angle * 0.6366197723675814 + 0.5)
    rest = angle - turns * 1.5703125
    rest = rest - turns * 4.837512969970703125e-4
    rest = rest - turns * 7.54978995489188216e-8
    quadrant = turns.astype(jnp.int32)
    square = rest * rest
    sine = rest + rest * square * (
        -1.6666654611e-1 + square * (8.3321608736e-3 + square * -1.9515295891e-4)
    )
    cosine = (1.0 - 0.5 * square) + square * square * (
        4.166664568298827e-2 + square * (-1.388731625493765e-3 + square * 2.443315711809948e-5)
    )
    odd = (quadrant & 1) == 1
    swapped_sine = jnp.where(odd, cosine, sine)
    swapped_cosine = jnp.where(odd, sine, cosine)
    sine = jnp.where((quadrant & 2) == 2, -swapped_sine, swapped_sine)
    cosine = jnp.where(((quadrant + 1) & 2) == 2, -swapped_cosine, swapped_cosine)
    return sine, cosine


def kernel(
    levels,
    images,
    matrix,
    offsets,
    tap_index,
    tap_table,
    phase_base,
    phase_slope,
    out,
    image,
    rows_of,
    params,
    outgoing,
    incoming,
    kept,
    windows,
    merged,
    handed,
    local_sem,
    first_sem,
    inter_sem,
    merge_sem,
    last_sem,
):
    width = image.shape[2]
    angles = image.shape[3]
    span = images.shape[3]
    share = rows_of.shape[1]
    tiles = share // LANES
    steps = width // REACH
    per_owner = span // REACH
    taps = tap_table.shape[0]
    scene = lax.axis_index("scene")
    aper = lax.axis_index("aper")
    core = lax.axis_index("range")
    other = 1 - core
    first_row = pl.multiple_of(core * share, share)
    other_row = pl.multiple_of(other * share, share)
    halves = [lax.rem(aper // 2**level, 2) for level in range(levels)]
    partners = [aper + (1 - 2 * halves[level]) * 2**level for level in range(levels)]

    barrier = pltpu.get_barrier_semaphore()
    for partner in partners:
        pl.semaphore_signal(barrier, inc=1, device_id=(scene, partner, core), device_id_type=MESH)
    pl.semaphore_signal(barrier, inc=1, device_id=(scene, aper, other), device_id_type=MESH)

    local_copies = [
        pltpu.make_async_copy(
            matrix.at[pl.ds(half * angles + first_row, share), :],
            rows_of.at[half],
            local_sem.at[half],
        )
        for half in range(2)
    ]
    for copy in local_copies:
        copy.start()

    own_range = pl.ds(pl.multiple_of(core * span, span), span)
    for part in range(2):
        image[0, part, own_range, :] = images[0, part].T

    for level in range(levels):
        picked = pl.ds(pl.multiple_of(halves[level] * angles + core * share, LANES), share)
        index = tap_index[level, :, picked]
        weights = [jnp.zeros(index.shape, F32) for _ in range(taps)]
        for entry in range(tap_table.shape[1]):
            hit = index == entry
            for tap in range(taps):
                weights[tap] = jnp.where(hit, tap_table[tap, entry], weights[tap])
        lines = weights + [
            offsets[level, :, picked].astype(F32) + float(REACH - 3),
            phase_base[level, :, picked],
            phase_slope[level, :, picked],
        ]
        for row, line in enumerate(lines):
            for slot in range(2):
                role = halves[level] if slot == 0 else 1 - halves[level]
                params[level, slot, row : row + 1, :] = jnp.where(
                    role == 0, line[0:1], line[1:2]
                )
        edge = jnp.zeros((2, REACH, share), BF16)
        for buffer in (incoming, kept):
            buffer[level, :, 0:REACH, :] = edge
            buffer[level, :, REACH + width : REACH + width + REACH, :] = edge

    pl.semaphore_wait(barrier, len(partners) + 1)

    def first_copy(place):
        return pltpu.make_async_remote_copy(
            src_ref=image.at[0, :, place, :],
            dst_ref=image.at[0, :, place, :],
            send_sem=first_sem.at[0],
            recv_sem=first_sem.at[1],
            device_id=(scene, aper, other),
            device_id_type=MESH,
        )

    def inter_copy(level, step):
        return pltpu.make_async_remote_copy(
            src_ref=outgoing.at[level, :, pl.ds(pl.multiple_of(step * REACH, REACH), REACH), :],
            dst_ref=incoming.at[
                level, :, pl.ds(pl.multiple_of((step + 1) * REACH, REACH), REACH), :
            ],
            send_sem=inter_sem.at[0, level, step],
            recv_sem=inter_sem.at[1, level, step],
            device_id=(scene, partners[level], core),
            device_id_type=MESH,
        )

    def merge_copy(level, step, row):
        place = image.at[
            level, :, pl.ds(pl.multiple_of(step * REACH, REACH), REACH), pl.ds(row, share)
        ]
        return pltpu.make_async_remote_copy(
            src_ref=place,
            dst_ref=place,
            send_sem=merge_sem.at[0, level - 1, step],
            recv_sem=merge_sem.at[1, level - 1, step],
            device_id=(scene, aper, other),
            device_id_type=MESH,
        )

    def last_copy(row):
        return pltpu.make_async_remote_copy(
            src_ref=handed,
            dst_ref=out.at[0, :, pl.ds(row, share), :],
            send_sem=last_sem.at[0],
            recv_sem=last_sem.at[1],
            device_id=(scene, aper, other),
            device_id_type=MESH,
        )

    def send(level, step):
        if level > 0:
            merge_copy(level, step, other_row).wait_recv()
        here = pl.ds(pl.multiple_of(step * REACH, REACH), REACH)
        there = pl.ds(pl.multiple_of((step + 1) * REACH, REACH), REACH)
        both = jnp.concatenate([image[level, part, here, :] for part in range(2)], axis=0)
        for slot in range(2):
            half = 1 - halves[level] if slot == 0 else halves[level]
            inter = lax.dot_general(
                both, rows_of[half], (((1,), (1,)), ((), ())), preferred_element_type=F32
            ).astype(BF16)
            for part in range(2):
                piece = inter[part * REACH : (part + 1) * REACH]
                if slot == 0:
                    outgoing[level, part, here, :] = piece
                else:
                    kept[level, part, there, :] = piece
            if slot == 0:
                inter_copy(level, step).start()

    def term(level, slot, step, tile):
        buffer = kept if slot == 0 else incoming
        columns = slice(tile * LANES, (tile + 1) * LANES)

        def line(row, count):
            return jnp.broadcast_to(params[level, slot, row : row + 1, columns], (count, LANES))

        amount = line(taps, 2 * REACH).astype(jnp.int32)
        weights = [line(tap, REACH) for tap in range(taps)]
        order = lax.broadcasted_iota(jnp.int32, (REACH, LANES), 0) + step * REACH
        sine, cosine = sincos(
            line(taps + 1, REACH) + line(taps + 2, REACH) * order.astype(F32)
        )
        shifted = []
        for part in range(2):
            value = buffer[
                level, part, pl.ds(pl.multiple_of(step * REACH, REACH), 3 * REACH), columns
            ].astype(F32)
            keep = 2 * REACH
            bit = REACH
            value = jnp.concatenate(
                [
                    jnp.where((amount & bit) == bit, value[bit:], value[:keep]),
                    value[keep : keep + FINE],
                ],
                axis=0,
            )
            while bit > FINE:
                bit //= 2
                keep = value.shape[0] - bit
                value = jnp.where((amount[:keep] & bit) == bit, value[bit:], value[:keep])
            while bit > 1:
                bit //= 2
                turned = pltpu.roll(value, value.shape[0] - bit, 0)
                value = jnp.where((amount[: value.shape[0]] & bit) == bit, turned, value)
            window = windows.at[tile, slot, part]
            window[...] = value
            total = weights[0] * value[:REACH]
            for tap in range(1, taps):
                total = total + weights[tap] * window[tap : tap + REACH, :]
            shifted.append(total)
        return (
            shifted[0] * cosine - shifted[1] * sine,
            shifted[0] * sine + shifted[1] * cosine,
        )

    def merge(level, step):
        @pl.when(step == 0)
        def _():
            inter_copy(level, 0).wait_recv()

        @pl.when(step + 1 < steps)
        def _():
            inter_copy(level, step + 1).wait_recv()

        here = pl.ds(pl.multiple_of(step * REACH, REACH), REACH)
        for tile in range(tiles):
            terms = [term(level, slot, step, tile) for slot in range(2)]
            for part in range(2):
                total = terms[0][part] + terms[1][part]
                if level + 1 < levels:
                    columns = pl.ds(pl.multiple_of(first_row + tile * LANES, LANES), LANES)
                    image[level + 1, part, here, columns] = total.astype(BF16)
                else:
                    merged[part, here, tile * LANES : (tile + 1) * LANES] = total
        if level + 1 < levels:
            merge_copy(level + 1, step, first_row).start()
        else:

            @pl.when(lax.rem(step, per_owner) == per_owner - 1)
            def _():
                owner = step // per_owner
                block = pl.ds(pl.multiple_of(owner * span, span), span)

                @pl.when(owner == core)
                def _():
                    for part in range(2):
                        out[0, part, pl.ds(first_row, share), :] = merged[part, block, :].T.astype(BF16)

                @pl.when(owner != core)
                def _():
                    for part in range(2):
                        handed[part] = merged[part, block, :].T.astype(BF16)
                    last_copy(first_row).start()

    first = first_copy(own_range)
    first.start()
    for copy in local_copies:
        copy.wait()
    first.wait_send()
    first_copy(pl.ds(pl.multiple_of(other * span, span), span)).wait_recv()

    @pl.loop(0, steps)
    def _(step):
        send(0, step)

    stages = [(merge, 0, 0)]
    lag = 0
    for level in range(1, levels):
        lag += SEND_LAG
        stages.append((send, level, lag))
        lag += MERGE_LAG - SEND_LAG
        stages.append((merge, level, lag))

    @pl.loop(0, steps + lag)
    def _(tick):
        for stage, level, late in stages:

            @pl.when((tick >= late) & (tick < late + steps))
            def _():
                stage(level, tick - late)

    @pl.loop(0, steps)
    def _(step):
        for level in range(levels):
            inter_copy(level, step).wait_send()
            if level > 0:
                merge_copy(level, step, first_row).wait_send()

    last = last_copy(first_row)
    last.wait_send()
    last_copy(other_row).wait_recv()


def body(images, interp_matrix, offsets, tap_index, tap_table, phase_base, phase_slope):
    cores = lax.axis_size("range")
    levels = offsets.shape[0]
    angles = images.shape[2]
    span = images.shape[3]
    width = span * cores
    share = angles // cores
    steps = width // REACH
    vmem = pl.BlockSpec(memory_space=pltpu.VMEM)
    anywhere = pl.BlockSpec(memory_space=pl.ANY)
    framed = width + 2 * REACH
    return pl.pallas_call(
        functools.partial(kernel, levels),
        out_shape=jax.ShapeDtypeStruct(images.shape, images.dtype),
        in_specs=[
            vmem,
            anywhere,
            vmem,
            vmem,
            pl.BlockSpec(memory_space=pltpu.SMEM),
            vmem,
            vmem,
        ],
        out_specs=vmem,
        scratch_shapes=[
            pltpu.VMEM((levels, 2, width, angles), BF16),
            pltpu.VMEM((2, share, angles), BF16),
            pltpu.VMEM((levels, 2, 16, share), F32),
            pltpu.VMEM((levels, 2, width, share), BF16),
            pltpu.VMEM((levels, 2, framed, share), BF16),
            pltpu.VMEM((levels, 2, framed, share), BF16),
            pltpu.VMEM((share // LANES, 2, 2, REACH + 2 * FINE, LANES), F32),
            pltpu.VMEM((2, width, share), F32),
            pltpu.VMEM((2, share, span), BF16),
            pltpu.SemaphoreType.DMA((2,)),
            pltpu.SemaphoreType.DMA((2,)),
            pltpu.SemaphoreType.DMA((2, levels, steps)),
            pltpu.SemaphoreType.DMA((2, levels - 1, steps)),
            pltpu.SemaphoreType.DMA((2,)),
        ],
        compiler_params=pltpu.CompilerParams(collective_id=0, has_side_effects=True),
    )(images, interp_matrix, offsets, tap_index, tap_table.T, phase_base, phase_slope)


def solution(mesh):
    return jax.shard_map(
        body,
        mesh=mesh,
        in_specs=(P(("scene", "aper"), None, None, "range"), P(), P(), P(), P(), P(), P()),
        out_specs=P(("scene", "aper"), None, None, "range"),
        check_vma=False,
    )
```

time: 82.7 us -> 38.1 us (0.46)
  waiting for transfers between devices: 39.6 us -> 0 us
  Pallas kernels: 0 us -> 36.3 us
  other arithmetic: 20.4 us -> 0 us
  starting transfers between devices: 11.4 us -> 0 us
  matrix products: 4.68 us -> 0 us
  local copies, waits for them, and re-layouts: 5.49 us -> 1.67 us
  between operations: 1 us -> 0.01 us
    ppermute x5 -> x0, waiting for transfers between devices: 39.6 us -> none  [the longest x3 39.6 us: from_partner(): return lax.ppermute(value, axis, pairs)]
    pallas_call x0 -> x1, Pallas kernels: none -> 36.3 us  [body(): pl.pallas_call(functools.partial(kernel, levels), out_shape=jax.ShapeDtyp...]
    ppermute x5 -> x0, starting transfers between devices: 11.4 us -> none  [the longest x3 7.65 us: from_partner(): return lax.ppermute(value, axis, pairs)]
    sub x2 -> x0, other arithmetic: 7.62 us -> none  [contribution(): real_part * cosine - imag_part * sine_part]
    select_n x36 -> x0, other arithmetic: 4.95 us -> none  [shifted(): moved = jnp.where(chosen_bits[None, :, None], rolled, moved)]
    add x8 -> x0, other arithmetic: 4.8 us -> none  [the longest x6 4.62 us: shifted(): summed + tap_rows[None, :, tap_number, None] * window[:, :, tap_number:ta...]
    dot_general x12 -> x0, matrix products: 4.68 us -> none  [the longest x6 2.82 us: interpolate(): jnp.einsum('pa,can->cpn', matrix_rows, image, preferred_element_type=jnp....]
    slice x47 -> x0, local copies, waits for them, and re-layouts: 3.01 us -> none  [the longest x36 2.81 us: shifted(): moved[:, :, stride_len:]]
  transfers between devices with their start and end apart: 5 -> 0, of which waited for: 3 -> 0; matrix products, arithmetic and copies ran while one was open for 9% -> 0% of each run, Pallas kernels for 0% -> 0%
where the time goes in v2:
time: 38.1 us; the launch traced here: 37.9 us
  Pallas kernels  36.3 us (95%)
  local copies, waits for them, and re-layouts  1.67 us (4%)
    pallas_call x1, Pallas kernels, body(): pl.pallas_call(functools.partial(kernel, levels), out_shape=jax.ShapeDtyp...  36.3 us
    unnamed x1, local copies, waits for them, and re-layouts  1.67 us

profile of v2, /device:TPU:0, one launch (start us, length us, event | category | flops | bytes accessed | tf_op | source)
XLA Modules:
  0.0 37.9 jit_solution(1447934571207752738)
XLA Ops:
  0.0 36.3 %shard_map.73 = bf16[1,2,512,128]{3,2,1,0:T(8,128)(2,1)} custom-call(bf16[1,2,512,128]{3,2,1,0:T(8,128)(2,1)} %images.1, bf16[1024,512]{1,0:T(8,128)(2,1)} %matrix.1, s32[3,2,1024]{2,1,0:T(2,128)} %offsets.1, s32[3,2,1024]{2,1,0:T(2,128)} %tap_index.1, f32[8,16]{1,0:T(8,128)} %bitcast.1, f32[3,2,1024]{2,1,0:T(2,128)} %phase_base.1, f32[3,2,1024]{2,1,0:T(2,128)} %phase_slope.1), custom_call_target="tpu_custom_call" | custom-call | tf_op jit(solution)/shard_map/pallas_call | solution.py:329
  36.3 1.7 %copy.9 = bf16[1,2,512,128]{3,2,1,0:T(8,128)(2,1)} copy(bf16[1,2,512,128]{3,2,1,0:T(8,128)(2,1)} %shard_map.73) | data formatting | bytes 524288

commit v3 on v2

--- a/solution.py
+++ b/solution.py
@@ -11,8 +11,8 @@
 LANES = 128
 REACH = 32
 FINE = 8
-SEND_LAG = 2
-MERGE_LAG = 7
+SEND_LAG = 1
+MERGE_LAG = 5
 F32 = jnp.float32
 BF16 = jnp.bfloat16
 
@@ -328,7 +328,7 @@
     framed = width + 2 * REACH
     return pl.pallas_call(
         functools.partial(kernel, levels),
-        out_shape=jax.ShapeDtypeStruct(images.shape, images.dtype),
+        out_shape=pltpu.VMEM(images.shape, images.dtype),
         in_specs=[
             vmem,
             anywhere,

time: 38.1 us -> 34.7 us (0.911)
  Pallas kernels: 36.3 us -> 33.8 us
  local copies, waits for them, and re-layouts: 1.67 us -> 0.71 us
    pallas_call x1, Pallas kernels: 36.3 us -> 33.8 us  [body(): pl.pallas_call(functools.partial(kernel, levels), out_shape=pltpu.VMEM(im...]
    unnamed x1, local copies, waits for them, and re-layouts: 1.67 us -> 0.71 us
where the time goes in v3:
time: 34.7 us; the launch traced here: 34.5 us
  Pallas kernels  33.8 us (97%)
  local copies, waits for them, and re-layouts  0.71 us (2%)
    pallas_call x1, Pallas kernels, body(): pl.pallas_call(functools.partial(kernel, levels), out_shape=pltpu.VMEM(im...  33.8 us
    unnamed x1, local copies, waits for them, and re-layouts  0.71 us

profile of v3, /device:TPU:0, one launch (start us, length us, event | category | flops | bytes accessed | tf_op | source)
XLA Modules:
  0.0 34.5 jit_solution(17510206439810910842)
XLA Ops:
  0.0 33.8 %shard_map.73 = bf16[1,2,512,128]{3,2,1,0:T(8,128)(2,1)S(1)} custom-call(bf16[1,2,512,128]{3,2,1,0:T(8,128)(2,1)} %images.1, bf16[1024,512]{1,0:T(8,128)(2,1)} %matrix.1, s32[3,2,1024]{2,1,0:T(2,128)} %offsets.1, s32[3,2,1024]{2,1,0:T(2,128)} %tap_index.1, f32[8,16]{1,0:T(8,128)} %bitcast.1, f32[3,2,1024]{2,1,0:T(2,128)} %phase_base.1, f32[3,2,1024]{2,1,0:T(2,128)} %phase_slope.1), custom_call_target="tpu_custom_call" | custom-call | tf_op jit(solution)/shard_map/pallas_call | solution.py:329
  33.8 0.7 %copy.9 = bf16[1,2,512,128]{3,2,1,0:T(8,128)(2,1)} copy(bf16[1,2,512,128]{3,2,1,0:T(8,128)(2,1)S(1)} %shard_map.73) | data formatting | bytes 524288
